TPU v7x, 512 devices: a whole 4x8x8 slice. The times are simulated.
512 devices in a mesh: fsdp: 64 (over y, z_lo, core), ctx: 8 (over x, z_hi).
Axes of the slice: x: 4, y: 8, z: 8 (z_hi: 2, z_lo: 4; z = z_hi * 4 + z_lo), core: 2. Of those that a mesh axis runs over, the one named last changes fastest.
Arguments:
- activations: bfloat16 [4096, 5120], P('fsdp', 'ctx'), may hold values from -500 to 500
- norm_gain: float32 [4096], P('fsdp'), may hold values from 0.25 to 1.75
- w_in: bfloat16 [3, 4096, 4096], P(None, 'fsdp'), may hold values from -0.09375 to 0.09375
- w_short: float32 [3, 4096, 3], P(None, 'fsdp'), may hold values from -3.5 to 3.5
- long_filter: bfloat16 [4096, 5120], P('fsdp'), may hold values from -1.1 to 1.1
- skip_gain: float32 [4096], P('fsdp'), may hold values from -4 to 4
- w_out: bfloat16 [4096, 4096], P('fsdp'), may hold values from -0.09375 to 0.09375
Outputs:
- mixer_out: bfloat16 [4096, 5120], P('fsdp', 'ctx')
All inputs are finite; a program needn't handle non-finite values.
Results may differ from a plain program's by a relative error of at most 0.035.
Values may be sent and summed in bfloat16 or wider, within the bound.
A program may use at most 64 MiB of HBM per device.

v0:
```python
import math

import jax
import jax.numpy as jnp
from jax import lax
from jax.sharding import PartitionSpec as P

epsilon = 1e-05
highest_precision = lax.Precision.HIGHEST


def shifted(block, axis, distance):
    devices = range(lax.axis_size(axis))
    route = [(i - distance, i) for i in devices if i - distance in devices]
    return lax.ppermute(block, axis, route)


def dft_tables(block_len):
    size = 2 * block_len
    sample = jnp.arange(size, dtype=jnp.int32)
    turns = sample[:, None] * sample[None, :] % size
    angle = turns.astype(jnp.float32) * (2.0 * math.pi / size)
    forward_pass = jnp.concatenate([jnp.cos(angle), -jnp.sin(angle)], axis=1)
    places = block_len + jnp.arange(block_len, dtype=jnp.int32)
    back_turns = sample[:, None] * places[None, :] % size
    back_angle = back_turns.astype(jnp.float32) * (2.0 * math.pi / size)
    inverse = jnp.concatenate([jnp.cos(back_angle), -jnp.sin(back_angle)], axis=0) / size
    return (forward_pass, inverse)


def complex_product(left, right):
    half = left.shape[-1] // 2
    left_re = left[..., :half]
    left_im = left[..., half:]
    right_re = right[..., :half]
    right_im = right[..., half:]
    return jnp.concatenate(
        [left_re * right_re - left_im * right_im, left_re * right_im + left_im * right_re], axis=-1
    )


def add_portion(running, portion, anchor, padded_spec, forward_pass, first_block, block_len):
    channels = portion.shape[0]
    count = portion.shape[1] // block_len
    local_blocks = running.shape[1]
    block_list = portion.astype(jnp.float32).reshape(channels, count, block_len)
    block_list = jnp.concatenate([block_list, jnp.zeros(block_list.shape, jnp.float32)], axis=2)
    filter_spectra = jnp.einsum(
        "grs,si->gri", block_list, forward_pass, precision=highest_precision
    )
    anchor_block = anchor // block_len

    def one_block(index, current):
        source = anchor_block + index
        spectrum = lax.dynamic_index_in_dim(filter_spectra, index, 1, keepdims=False)

        def apply_block(inner):
            start = local_blocks + first_block - source
            chosen = lax.dynamic_slice_in_dim(padded_spec, start, local_blocks, 1)
            return inner + complex_product(chosen, spectrum[:, None, :])

        def keep_block(inner):
            return inner

        return lax.cond(source < first_block + local_blocks, apply_block, keep_block, current)

    return lax.fori_loop(0, count, one_block, running)


def shards(activations, norm_gain, w_in, w_short, long_filter, skip_gain, w_out):
    channels = activations.shape[0]
    tok_rows = activations.shape[1]
    gathered, gains = (
        lax.all_gather(activations, "fsdp", axis=0, tiled=True),
        lax.all_gather(norm_gain.astype(jnp.bfloat16), "fsdp", axis=0, tiled=True).astype(
            norm_gain.dtype
        ),
    )
    factor = lax.rsqrt(jnp.mean(jnp.square(gathered.astype(jnp.float32)), axis=0) + epsilon)
    normed = (gathered.astype(jnp.float32) * factor[None, :] * gains[:, None]).astype(jnp.bfloat16)
    projected = jnp.einsum("sci,it->sct", w_in, normed, preferred_element_type=jnp.float32)
    projected = projected.astype(jnp.bfloat16)
    taps = w_short.shape[2]
    earlier = shifted(projected[:, :, tok_rows - (taps - 1) :], "ctx", 1)
    padded = jnp.concatenate([earlier, projected], axis=2).astype(jnp.float32)
    smoothed = jnp.zeros((3, channels, tok_rows), jnp.float32)
    for tap_index in range(taps):
        begin = taps - 1 - tap_index
        smoothed = (
            smoothed + w_short[:, :, tap_index][:, :, None] * padded[:, :, begin : begin + tok_rows]
        )
    query = smoothed[0]
    gated = (smoothed[1] * smoothed[2]).astype(jnp.bfloat16)
    block_len = 128
    local_blocks = tok_rows // block_len
    total_len = long_filter.shape[1]
    total_blocks = total_len // block_len
    forward_pass, inverse = dft_tables(block_len)
    edge = jnp.zeros((channels, block_len), jnp.float32)
    filter_wide = jnp.concatenate([edge, long_filter.astype(jnp.float32), edge], axis=1)
    filter_rows = filter_wide.reshape(channels, total_blocks + 2, block_len)
    segments = jnp.concatenate(
        [filter_rows[:, :total_blocks], filter_rows[:, 1 : total_blocks + 1]], axis=2
    )
    filter_spec = jnp.einsum("ckn,nf->ckf", segments, forward_pass, precision=highest_precision)
    padded_spec = jnp.concatenate(
        [jnp.zeros((channels, local_blocks, filter_spec.shape[2]), jnp.float32), filter_spec],
        axis=1,
    )
    my_index = lax.axis_index("ctx")
    first_token = my_index * tok_rows
    first_block = my_index * local_blocks
    empty = jnp.zeros((channels, local_blocks, 4 * block_len), jnp.float32)
    cycle_size = lax.axis_size("ctx")
    running = add_portion(
        empty, gated, first_token, padded_spec, forward_pass, first_block, block_len
    )

    def turn(turn_index, carried):
        current, moving = carried
        moving = shifted(moving, "ctx", 1)
        source = (my_index - turn_index + cycle_size) % cycle_size
        current = add_portion(
            current, moving, source * tok_rows, padded_spec, forward_pass, first_block, block_len
        )
        return (current, moving)

    accumulated, moved = lax.fori_loop(1, cycle_size, turn, (running, gated))
    filtered = jnp.einsum("caf,fi->cai", accumulated, inverse, precision=highest_precision).reshape(
        channels, tok_rows
    )
    mixed = (query * (filtered + skip_gain[:, None] * gated.astype(jnp.float32))).astype(
        jnp.bfloat16
    )
    result = jnp.dot(
        w_out, lax.all_gather(mixed, "fsdp", axis=0, tiled=True), preferred_element_type=jnp.float32
    )
    return result.astype(jnp.bfloat16)


def solution(mesh):
    placed = (
        P("fsdp", "ctx"),
        P("fsdp"),
        P(None, "fsdp", None),
        P(None, "fsdp", None),
        P("fsdp", None),
        P("fsdp"),
        P("fsdp", None),
    )
    return jax.shard_map(
        shards, mesh=mesh, in_specs=placed, out_specs=P("fsdp", "ctx"), check_vma=False
    )
```

profile of v0, /device:TPU:1, one launch (start us, length us, event | category | flops | bytes accessed | tf_op | source)
XLA Modules:
  0.0 507.4 jit_solution(1813700334814015170)
XLA Ops:
  8.0 1.3 dynamic-slice
  10.3 143.0 %all-reduce.3 = bf16[4096]{0:T(1024)(128)(2,1)S(1)} all-reduce(bf16[4096]{0:T(1024)(128)(2,1)S(1)} %dynamic-update-slice), channel_id=1, replica_groups=mesh['fsdp'=64,'ctx'=8] {'fsdp'}, use_global_device_ids=true, to_apply=%add.3 | all-reduce | flops 4096 | bytes 16384
  154.5 1.2 pad_maximum_fusion
  155.6 1.5 reshape.42
  159.1 1.2 fusion.49
  160.6 6.0 %fusion.10 = f32[64,40,512]{2,1,0:T(8,128)} fusion(f32[64,40,128]{2,1,0:T(8,128)S(1)} %get-tuple-element.735, f32[64,40,128]{2,1,0:T(8,128)S(1)} %get-tuple-element.734, f32[256,256]{1,0:T(8,128)S(1)} %get-tuple-element.741, f32[256,256]{1,0:T(8,128)S(1)} %get-tuple-element.742), kind=kOutput, calls=%fused_computation.22 | convolution fusion | flops 4027318272 | bytes 8388608 | tf_op jit(solution)/shard_map/ckn,nf->ckf/dot_general | solution.py:105
  166.6 3.7 fusion.4
  170.7 2.0 fusion.17
  172.8 6.3 %collective-permute-start.1 = (bf16[3,64,2]{2,1,0:T(8,128)(2,1)S(1)}, bf16[3,64,2]{2,1,0:T(8,128)(2,1)S(1)}, u32[]{:S(2)}, u32[]{:S(2)}) collective-permute-start(bf16[3,64,2]{2,1,0:T(8,128)(2,1)S(1)} %slice.88), channel_id=1, source_target_pairs={{0,1},{1,2},{2,3},{3,4},{4,5},{5,6},{6,7},{8,9},{9,10},{10,11},{11... | collective-permute-start | bytes 2312 | tf_op jit(solution)/shard_map/ppermute | solution.py:15
  179.1 6.1 %concatenate.44 = f32[64,45,512]{2,1,0:T(8,128)} pad(f32[64,40,512]{2,1,0:T(8,128)} %fusion.10, f32[]{:T(128)} %constant.250.clone.1), padding=0_0x5_0x0_0 | pad | bytes 11141124 | tf_op jit(solution)/shard_map/concatenate | solution.py:106
  186.8 1.3 fusion.22
  188.3 15.8 %while.67 = (s32[]{:T(128)}, f32[64,5,512]{2,1,0:T(8,128)S(1)}, s32[]{:T(128)}, s32[]{:T(128)}, s32[]{:T(128)}, /*index=5*/f32[64,45,512]{2,1,0:T(8,128)}, f32[64,5,512]{2,0,1:T(8,128)}, s32[]{:T(128)}) while((s32[]{:T(128)}, f32[64,5,512]{2,1,0:T(8,128)S(1)}, s32[]{:T(128)}, s32[]{:T(128)}, s32[]{:T(128)}, ...), condition=%wide.region_4.5_spmd, body=%wide.region_1.4_spmd.sunk | while | flops 819214 | bytes 3670303 | solution.py:67
  188.3 3.1 conditional.4
  189.2 1.8 multiply_subtract_fusion
  191.5 3.1 conditional.4
  192.4 1.8 multiply_subtract_fusion
  194.6 3.1 conditional.4
  195.5 1.8 multiply_subtract_fusion
  197.8 3.1 conditional.4
  198.7 1.8 multiply_subtract_fusion
  200.9 3.1 conditional.4
  201.9 1.8 multiply_subtract_fusion
  204.1 104.4 %while.69 = (s32[]{:T(128)}, f32[64,5,512]{2,1,0:T(8,128)S(1)}, bf16[64,640]{1,0:T(8,128)(2,1)S(1)}, s32[]{:T(128)}, f32[256,512]{1,0:T(8,128)}, /*index=5*/s32[...) while((s32[]{:T(128)}, f32[64,5,512]{2,1,0:T(8,128)S(1)}, ...), condition=%wide.region_10.11_spmd, body=%wide.region_5.10_spmd.sunk | while | flops 504135712 | bytes 5587787 | solution.py:128
  204.1 2.4 collective-permute-start
  206.6 2.2 collective-permute-done
  208.8 1.5 fusion.68
  210.6 19.0 %collective-permute-start = (bf16[64,640]{1,0:T(8,128)(2,1)S(1)}, bf16[64,640]{1,0:T(8,128)(2,1)S(1)}, u32[]{:S(2)}, u32[]{:S(2)}) collective-permute-start(bf16[64,640]{1,0:T(8,128)(2,1)S(1)} %get-tuple-element.963), channel_id=1, source_target_pairs={{0,1},{1,2},{2,3},{3,4},{4,5},{5,6},{6,7},{8,9},{9,10},{10,11},{11... | collective-permute-start | bytes 245768 | tf_op jit(solution)/shard_map/while/body/eval_jaxpr/ppermute | solution.py:15
  229.6 1.4 collective-permute-done
  231.0 1.5 fusion.68
  232.8 7.8 %collective-permute-start = (bf16[64,640]{1,0:T(8,128)(2,1)S(1)}, bf16[64,640]{1,0:T(8,128)(2,1)S(1)}, u32[]{:S(2)}, u32[]{:S(2)}) collective-permute-start(bf16[64,640]{1,0:T(8,128)(2,1)S(1)} %get-tuple-element.963), channel_id=1, source_target_pairs={{0,1},{1,2},{2,3},{3,4},{4,5},{5,6},{6,7},{8,9},{9,10},{10,11},{11... | collective-permute-start | bytes 245768 | tf_op jit(solution)/shard_map/while/body/eval_jaxpr/ppermute | solution.py:15
  240.7 1.4 collective-permute-done
  242.1 1.5 fusion.68
  243.9 19.9 %collective-permute-start = (bf16[64,640]{1,0:T(8,128)(2,1)S(1)}, bf16[64,640]{1,0:T(8,128)(2,1)S(1)}, u32[]{:S(2)}, u32[]{:S(2)}) collective-permute-start(bf16[64,640]{1,0:T(8,128)(2,1)S(1)} %get-tuple-element.963), channel_id=1, source_target_pairs={{0,1},{1,2},{2,3},{3,4},{4,5},{5,6},{6,7},{8,9},{9,10},{10,11},{11... | collective-permute-start | bytes 245768 | tf_op jit(solution)/shard_map/while/body/eval_jaxpr/ppermute | solution.py:15
  263.8 1.4 collective-permute-done
  265.3 1.5 fusion.68
  267.1 8.7 %collective-permute-start = (bf16[64,640]{1,0:T(8,128)(2,1)S(1)}, bf16[64,640]{1,0:T(8,128)(2,1)S(1)}, u32[]{:S(2)}, u32[]{:S(2)}) collective-permute-start(bf16[64,640]{1,0:T(8,128)(2,1)S(1)} %get-tuple-element.963), channel_id=1, source_target_pairs={{0,1},{1,2},{2,3},{3,4},{4,5},{5,6},{6,7},{8,9},{9,10},{10,11},{11... | collective-permute-start | bytes 245768 | tf_op jit(solution)/shard_map/while/body/eval_jaxpr/ppermute | solution.py:15
  275.8 1.4 collective-permute-done
  277.2 1.5 fusion.68
  279.0 12.3 %collective-permute-start = (bf16[64,640]{1,0:T(8,128)(2,1)S(1)}, bf16[64,640]{1,0:T(8,128)(2,1)S(1)}, u32[]{:S(2)}, u32[]{:S(2)}) collective-permute-start(bf16[64,640]{1,0:T(8,128)(2,1)S(1)} %get-tuple-element.963), channel_id=1, source_target_pairs={{0,1},{1,2},{2,3},{3,4},{4,5},{5,6},{6,7},{8,9},{9,10},{10,11},{11... | collective-permute-start | bytes 245768 | tf_op jit(solution)/shard_map/while/body/eval_jaxpr/ppermute | solution.py:15
  291.3 1.4 collective-permute-done
  292.8 1.5 fusion.68
  294.6 9.8 %collective-permute-start = (bf16[64,640]{1,0:T(8,128)(2,1)S(1)}, bf16[64,640]{1,0:T(8,128)(2,1)S(1)}, u32[]{:S(2)}, u32[]{:S(2)}) collective-permute-start(bf16[64,640]{1,0:T(8,128)(2,1)S(1)} %get-tuple-element.963), channel_id=1, source_target_pairs={{0,1},{1,2},{2,3},{3,4},{4,5},{5,6},{6,7},{8,9},{9,10},{10,11},{11... | collective-permute-start | bytes 245768 | tf_op jit(solution)/shard_map/while/body/eval_jaxpr/ppermute | solution.py:15
  304.5 2.2 collective-permute-done
  306.7 1.5 fusion.68
  308.5 1.9 convolution_bitcast_fusion
  310.4 1.8 fusion.38
  312.3 184.0 %all-gather.5.cloned.1.call-done = bf16[4096,640]{1,0:T(8,128)(2,1)} async-done(((bf16[64,640]{1,0:T(8,128)(2,1)}), bf16[4096,640]{1,0:T(8,128)(2,1)}) %all-gather.5.cloned.1.call-update) | async-done | bytes 5242896 | tf_op jit(solution)/shard_map/all_gather | solution.py:136
  496.3 4.3 fusion.20
  (108 shorter events, 15.7 us)
Async XLA Ops:
  6.5 163.8 %copy-start = (bf16[3,64,4096]{2,1,0:T(8,128)(2,1)S(1)}, bf16[3,64,4096]{2,1,0:T(8,128)(2,1)}, u32[]{:S(2)}) copy-start(bf16[3,64,4096]{2,1,0:T(8,128)(2,1)} %param.19) | copy-start | bytes 4718596
  6.5 160.1 %all-gather.3.cloned.1.call-start = ((), (), s32[]{:S(2)}) async-start(), calls=%async_computation | async-start | bytes 5324800 | tf_op jit(solution)/shard_map/all_gather | solution.py:74
  7.3 489.0 %all-gather.5.cloned.1.call-start = ((), (), s32[]{:S(2)}) async-start(), calls=%async_computation.1 | async-start | bytes 5324800 | tf_op jit(solution)/shard_map/all_gather | solution.py:136
  155.6 3.5 copy-start.5
  158.2 2.4 copy-start.3
  166.6 4.0 copy-start.2
  172.8 12.5 %collective-permute-start.1 = (bf16[3,64,2]{2,1,0:T(8,128)(2,1)S(1)}, bf16[3,64,2]{2,1,0:T(8,128)(2,1)S(1)}, u32[]{:S(2)}, u32[]{:S(2)}) collective-permute-start(bf16[3,64,2]{2,1,0:T(8,128)(2,1)S(1)} %slice.88), channel_id=1, source_target_pairs={{0,1},{1,2},{2,3},{3,4},{4,5},{5,6},{6,7},{8,9},{9,10},{10,11},{11... | collective-permute-start | bytes 2312 | tf_op jit(solution)/shard_map/ppermute | solution.py:15
  185.3 1.5 copy-start.4
  185.9 0.8 copy-start.1
  204.1 106.3 %copy-start.6 = (f32[64]{0:T(128)S(1)}, f32[64]{0:T(128)}, u32[]{:S(2)}) copy-start(f32[64]{0:T(128)} %param.22) | copy-start | bytes 772
  204.1 4.7 collective-permute-start
  210.6 20.4 %collective-permute-start = (bf16[64,640]{1,0:T(8,128)(2,1)S(1)}, bf16[64,640]{1,0:T(8,128)(2,1)S(1)}, u32[]{:S(2)}, u32[]{:S(2)}) collective-permute-start(bf16[64,640]{1,0:T(8,128)(2,1)S(1)} %get-tuple-element.963), channel_id=1, source_target_pairs={{0,1},{1,2},{2,3},{3,4},{4,5},{5,6},{6,7},{8,9},{9,10},{10,11},{11... | collective-permute-start | bytes 245768 | tf_op jit(solution)/shard_map/while/body/eval_jaxpr/ppermute | solution.py:15
  232.8 9.2 %collective-permute-start = (bf16[64,640]{1,0:T(8,128)(2,1)S(1)}, bf16[64,640]{1,0:T(8,128)(2,1)S(1)}, u32[]{:S(2)}, u32[]{:S(2)}) collective-permute-start(bf16[64,640]{1,0:T(8,128)(2,1)S(1)} %get-tuple-element.963), channel_id=1, source_target_pairs={{0,1},{1,2},{2,3},{3,4},{4,5},{5,6},{6,7},{8,9},{9,10},{10,11},{11... | collective-permute-start | bytes 245768 | tf_op jit(solution)/shard_map/while/body/eval_jaxpr/ppermute | solution.py:15
  243.9 21.3 %collective-permute-start = (bf16[64,640]{1,0:T(8,128)(2,1)S(1)}, bf16[64,640]{1,0:T(8,128)(2,1)S(1)}, u32[]{:S(2)}, u32[]{:S(2)}) collective-permute-start(bf16[64,640]{1,0:T(8,128)(2,1)S(1)} %get-tuple-element.963), channel_id=1, source_target_pairs={{0,1},{1,2},{2,3},{3,4},{4,5},{5,6},{6,7},{8,9},{9,10},{10,11},{11... | collective-permute-start | bytes 245768 | tf_op jit(solution)/shard_map/while/body/eval_jaxpr/ppermute | solution.py:15
  267.1 10.1 %collective-permute-start = (bf16[64,640]{1,0:T(8,128)(2,1)S(1)}, bf16[64,640]{1,0:T(8,128)(2,1)S(1)}, u32[]{:S(2)}, u32[]{:S(2)}) collective-permute-start(bf16[64,640]{1,0:T(8,128)(2,1)S(1)} %get-tuple-element.963), channel_id=1, source_target_pairs={{0,1},{1,2},{2,3},{3,4},{4,5},{5,6},{6,7},{8,9},{9,10},{10,11},{11... | collective-permute-start | bytes 245768 | tf_op jit(solution)/shard_map/while/body/eval_jaxpr/ppermute | solution.py:15
  279.0 13.8 %collective-permute-start = (bf16[64,640]{1,0:T(8,128)(2,1)S(1)}, bf16[64,640]{1,0:T(8,128)(2,1)S(1)}, u32[]{:S(2)}, u32[]{:S(2)}) collective-permute-start(bf16[64,640]{1,0:T(8,128)(2,1)S(1)} %get-tuple-element.963), channel_id=1, source_target_pairs={{0,1},{1,2},{2,3},{3,4},{4,5},{5,6},{6,7},{8,9},{9,10},{10,11},{11... | collective-permute-start | bytes 245768 | tf_op jit(solution)/shard_map/while/body/eval_jaxpr/ppermute | solution.py:15
  294.6 12.1 %collective-permute-start = (bf16[64,640]{1,0:T(8,128)(2,1)S(1)}, bf16[64,640]{1,0:T(8,128)(2,1)S(1)}, u32[]{:S(2)}, u32[]{:S(2)}) collective-permute-start(bf16[64,640]{1,0:T(8,128)(2,1)S(1)} %get-tuple-element.963), channel_id=1, source_target_pairs={{0,1},{1,2},{2,3},{3,4},{4,5},{5,6},{6,7},{8,9},{9,10},{10,11},{11... | collective-permute-start | bytes 245768 | tf_op jit(solution)/shard_map/while/body/eval_jaxpr/ppermute | solution.py:15
Sparse Core Ops, SparseCore 0:
  9.5 128.2 all-gather.2
  312.4 183.8 all-gather.4
where the time goes:
time: 510 us; the launch traced here: 507 us
  waiting for transfers between devices  196 us (38%)
  blocking collectives  143 us (28%)
  starting transfers between devices  86.1 us (17%)
  matrix products  26.3 us (5%)
  other arithmetic  23.3 us (5%)
  local copies, waits for them, and re-layouts  15.4 us (3%)
  between operations  14.3 us (3%)
    all_gather x1, waiting for transfers between devices, shards(): lax.all_gather(mixed, 'fsdp', axis=0, tiled=True)  184 us
    unnamed x1, blocking collectives  143 us
    ppermute x8, starting transfers between devices, shifted(): return lax.ppermute(block, axis, route)  86.1 us
    dot_general x8, matrix products, add_portion(): jnp.einsum('grs,si->gri', block_list, forward_pass, precision=highest_pre...  12 us
    ppermute x8, waiting for transfers between devices, shifted(): return lax.ppermute(block, axis, route)  11.5 us
  transfers between devices with their start and end apart: 10, of which 8 were waited for; matrix products, arithmetic and copies ran while one was open for 4% of the time, Pallas kernels for 0%

commit v1 on v0

v1 whole, which is shorter than its diff:
```python
import functools

import jax
import jax.numpy as jnp
from jax import lax
from jax.experimental import pallas as pl
from jax.experimental.pallas import tpu as pltpu
from jax.sharding import PartitionSpec as P

EPSILON = 1e-05
MESH = pl.DeviceIdType.MESH
LANES = 128
ROWS = 8


class Plan:
    def __init__(self, fsdp, ctx, rows, tokens, long_len):
        self.cores = 2
        self.ring = {64: 8, 16: 4, 8: 4}[fsdp]
        self.line = fsdp // (self.ring * self.cores)
        self.plane = self.line * self.cores
        self.fsdp, self.ctx = fsdp, ctx
        self.rows, self.tokens, self.long_len = rows, tokens, long_len
        self.half = self.ring // 2
        self.blocks = long_len // LANES
        self.token_tiles = tokens // LANES


def copy_to(src, dst, send, recv, device):
    return pltpu.make_async_remote_copy(
        src_ref=src, dst_ref=dst, send_sem=send, recv_sem=recv, device_id=device, device_id_type=MESH
    )


def kernel(
    plan, act, gain, w_in, w_short, filt, skip, w_out, out,
    gath, mixg, win, wout, xin, hin, hrow, tmat, acc, acc2, plane_sum, ring_sum,
    pbuf, rbuf, mbuf, mrecv, seq, gseq, fseq, skipb,
    lsem, plane_sem, ring_sem, zsem, ysem, csem, zsem2, ysem2, csem2, asem, bsem,
):
    me = lax.axis_index("fsdp")
    ctx = lax.axis_index("ctx")
    ring, line, plane, half = plan.ring, plan.line, plan.plane, plan.half
    y = me // plane
    p = lax.rem(me, plane)
    z = p // plan.cores
    core = lax.rem(p, plan.cores)
    rows, tokens = plan.rows, plan.tokens

    def at(yy, zz, cc):
        return (yy * line + zz) * plan.cores + cc

    def turn(yy):
        return lax.rem(yy + 2 * ring, ring)

    loads = [
        pltpu.make_async_copy(act, xin, lsem.at[0]),
        pltpu.make_async_copy(filt.at[ctx], hin, lsem.at[1]),
        pltpu.make_async_copy(w_in, win, lsem.at[2]),
        pltpu.make_async_copy(w_out, wout, lsem.at[3]),
    ]
    for load in loads:
        load.start()

    barrier = pltpu.get_barrier_semaphore()

    def greet(device):
        pl.semaphore_signal(barrier, inc=1, device_id=device, device_id_type=MESH)

    @pl.loop(1, plane)
    def _(o):
        greet({"fsdp": y * plane + (p ^ o)})

    @pl.loop(1, ring)
    def _(o):
        greet({"fsdp": turn(y + o) * plane + p})

    if plan.ctx > 1:
        @pl.loop(1, plan.ctx)
        def _(o):
            greet({"ctx": ctx ^ o})

    def column(row):
        n = row.shape[1]
        same = lax.broadcasted_iota(jnp.int32, (n, n), 0) == lax.broadcasted_iota(jnp.int32, (n, n), 1)
        return jnp.sum(jnp.where(same, jnp.broadcast_to(row, (n, n)), 0.0), axis=1, keepdims=True)

    loads[0].wait()
    own = xin[...].astype(jnp.float32)
    gath[me] = (own * column(gain[...])).astype(jnp.bfloat16)
    squares = jnp.sum(own * own, axis=0, keepdims=True)
    plane_sum[0] = jnp.zeros((ROWS, LANES), jnp.float32)
    for k in range(plan.token_tiles):
        plane_sum[0, k : k + 1, :] = squares[:, k * LANES : (k + 1) * LANES]
    skipb[...] = jnp.broadcast_to(column(skip[...]), (rows, LANES))
    acc[...] = jnp.zeros_like(acc)
    acc2[...] = jnp.zeros_like(acc2)
    gseq[...] = jnp.zeros_like(gseq)
    seq[:, :, :LANES] = jnp.zeros((3, ROWS, LANES), jnp.float32)
    pl.semaphore_wait(barrier, (plane - 1) + (ring - 1) + (plan.ctx - 1))

    def plane_copy(o):
        return copy_to(
            plane_sum.at[0], plane_sum.at[o], plane_sem.at[0, o], plane_sem.at[1, o], {"fsdp": y * plane + (p ^ o)}
        )

    def ring_copy(o):
        return copy_to(
            ring_sum.at[0], ring_sum.at[o], ring_sem.at[0, o], ring_sem.at[1, o], {"fsdp": turn(y + o) * plane + p}
        )

    def gather(buf, zs, ys, cs, multiply, fillers):
        def zcopy(o, zz_from):
            block = buf.at[at(y, zz_from, core)]
            return copy_to(block, block, zs.at[0, o], zs.at[1, o], {"fsdp": at(y, z ^ o, core)})

        def origin(d, s):
            return turn(y - s) if d == 0 else turn(y + s)

        def part(block, d, s):
            if s < half:
                return buf.at[block]
            return buf.at[block, pl.ds(d * (rows // 2), rows // 2)]

        def ycopy(d, s, o, receive):
            came = s if receive else s - 1
            block = at(origin(d, came), z ^ o, core)
            view = part(block, d, s)
            to = turn(y + 1) if d == 0 else turn(y - 1)
            return copy_to(view, view, ys.at[0, d, s - 1, o], ys.at[1, d, s - 1, o], {"fsdp": at(to, z, core)})

        def ccopy(d, s, o, mine):
            r = s + d * half
            block = at(origin(d, s), z ^ o, core if mine else 1 - core)
            view = part(block, d, s)
            return copy_to(view, view, cs.at[0, r, o], cs.at[1, r, o], {"fsdp": at(y, z, 1 - core)})

        for o in range(1, line):
            zcopy(o, z).start()
        for d in range(2):
            ycopy(d, 1, 0, False).start()
        ccopy(0, 0, 0, True).start()
        fillers[0]()
        for o in range(1, line):
            zcopy(o, z ^ o).wait_recv()
            for d in range(2):
                ycopy(d, 1, o, False).start()
            ccopy(0, 0, o, True).start()
        fillers[1]()
        for s in range(1, half + 1):
            @pl.loop(0, line)
            def _(o):
                for d in range(2):
                    ycopy(d, s, o, True).wait_recv()
                    if s < half:
                        ycopy(d, s + 1, o, False).start()
                    ccopy(d, s, o, True).start()

            @pl.loop(0, line)
            def _(o):
                for d in range(2 if s > 1 else 1):
                    ccopy(d, s - 1, o, False).wait_recv()

            for d in range(2 if s > 1 else 1):
                multiply(origin(d, s - 1))
            fillers[1 + s]()

        @pl.loop(0, line)
        def _(o):
            for d in range(2):
                ccopy(d, half, o, False).wait_recv()

        multiply(origin(0, half))

        def drain():
            for o in range(1, line):
                zcopy(o, z).wait_send()

            @pl.loop(0, line)
            def _(o):
                ccopy(0, 0, o, True).wait_send()
                for s in range(1, half + 1):
                    for d in range(2):
                        ycopy(d, s, o, False).wait_send()
                        ccopy(d, s, o, True).wait_send()

        return drain

    width = plane * rows

    def multiply_in(yy):
        w = win[:, :, pl.ds(pl.multiple_of(yy * width, width), width)].reshape(3 * rows, width)
        x = gath[pl.ds(yy * plane, plane)].reshape(width, tokens)
        acc[...] += jnp.dot(w, x, preferred_element_type=jnp.float32)

    def multiply_out(yy):
        w = wout[:, pl.ds(pl.multiple_of(yy * width, width), width)]
        x = mixg[pl.ds(yy * plane, plane)].reshape(width, tokens)
        acc2[...] += jnp.dot(w, x, preferred_element_type=jnp.float32)

    def spread_filter():
        for load in loads[1:]:
            load.wait()
        h = hin[...].astype(jnp.float32)
        for d in range(plan.blocks):
            hrow[pl.ds(d, ROWS, stride=plan.blocks), :] = h[:, d * LANES : (d + 1) * LANES]

    later = lax.broadcasted_iota(jnp.int32, (LANES, LANES), 1) >= lax.broadcasted_iota(jnp.int32, (LANES, LANES), 0)

    def band(first, last):
        @pl.loop(first, last)
        def _(c):
            def body(d, before):
                r = c * plan.blocks + d
                line_ = jnp.broadcast_to(hrow[pl.ds(r, 1), :], (LANES, LANES))
                rolled = pltpu.roll(line_, 0, 1, stride=1, stride_axis=0)
                tmat[r] = jnp.where(later, rolled, before).astype(jnp.bfloat16)
                return rolled

            lax.fori_loop(0, plan.blocks, body, jnp.zeros((LANES, LANES), jnp.float32))

    def start_plane():
        @pl.loop(1, plane)
        def _(o):
            plane_copy(o).start()

        spread_filter()

    def start_ring():
        @pl.loop(1, plane)
        def _(o):
            plane_copy(o).wait_recv()

        ring_sum[0] = jnp.sum(plane_sum[...], axis=0)

        @pl.loop(1, ring)
        def _(o):
            ring_copy(o).start()

        band(0, 2)

    bands = [functools.partial(band, 2 + 6 * i // half, 2 + 6 * (i + 1) // half) for i in range(half)]
    drain1 = gather(gath, zsem, ysem, csem, multiply_in, [start_plane, start_ring] + bands)

    @pl.loop(1, ring)
    def _(o):
        ring_copy(o).wait_recv()

    features = plan.fsdp * rows
    factor = lax.rsqrt(jnp.sum(ring_sum[...], axis=0) / features + EPSILON)
    for k in range(plan.token_tiles):
        lanes = slice(k * LANES, (k + 1) * LANES)
        for s in range(3):
            scaled = acc[s * rows : (s + 1) * rows, lanes] * factor[k : k + 1, :]
            for j in range(plan.ctx):
                n = rows // plan.ctx
                pbuf[j, s, :, lanes] = scaled[j * n : (j + 1) * n].astype(jnp.bfloat16)

    def swap(src, dst, sem):
        def one(o):
            return copy_to(src.at[ctx ^ o], dst.at[ctx], sem.at[0, o], sem.at[1, o], {"ctx": ctx ^ o})

        def arrival(o):
            return copy_to(src.at[ctx ^ o], dst.at[ctx ^ o], sem.at[0, o], sem.at[1, o], {"ctx": ctx ^ o})

        if plan.ctx > 1:
            @pl.loop(1, plan.ctx)
            def _(o):
                one(o).start()

        dst[ctx] = src[ctx]
        if plan.ctx > 1:
            @pl.loop(1, plan.ctx)
            def _(o):
                arrival(o).wait_recv()

        def drain():
            if plan.ctx > 1:
                @pl.loop(1, plan.ctx)
                def _(o):
                    one(o).wait_send()

        return drain

    drain2 = swap(pbuf, rbuf, asem)

    for j in range(plan.ctx):
        for s in range(3):
            seq[s, :, LANES + j * tokens : LANES + (j + 1) * tokens] = rbuf[j, s].astype(jnp.float32)

    def smooth(s):
        taps = w_short[s, ctx]
        full = seq[s]
        total = taps[:, 0:1] * full + taps[:, 1:2] * pltpu.roll(full, 1, 1)
        total = total + taps[:, 2:3] * pltpu.roll(full, 2, 1)
        return total[:, LANES:]

    gated = (smooth(1) * smooth(2)).astype(jnp.bfloat16).astype(jnp.float32)
    query = smooth(0)
    blocks = plan.blocks
    for b in range(blocks):
        gseq[pl.ds(blocks + b, ROWS, stride=2 * blocks), :] = gated[:, b * LANES : (b + 1) * LANES]

    @pl.loop(0, ROWS)
    def _(c):
        base = c * 2 * blocks + blocks
        lhs = jnp.concatenate(
            [gseq[pl.ds(base - d, blocks), :].astype(jnp.bfloat16) for d in range(blocks)], axis=1
        )
        rhs = tmat[pl.ds(c * blocks, blocks)].reshape(blocks * LANES, LANES)
        fseq[pl.ds(c * blocks, blocks), :] = jnp.dot(lhs, rhs, preferred_element_type=jnp.float32)

    direct = skipb[pl.ds(ctx * ROWS, ROWS), :]
    for b in range(blocks):
        lanes = slice(b * LANES, (b + 1) * LANES)
        value = query[:, lanes] * (fseq[pl.ds(b, ROWS, stride=blocks), :] + direct * gated[:, lanes])
        j, k = b // plan.token_tiles, b % plan.token_tiles
        mbuf[j, :, k * LANES : (k + 1) * LANES] = value.astype(jnp.bfloat16)

    drain3 = swap(mbuf, mrecv, bsem)
    mixg[me] = mrecv[...].astype(jnp.float32).reshape(rows, tokens).astype(jnp.bfloat16)

    nothing = [lambda: None] * (half + 2)
    drain4 = gather(mixg, zsem2, ysem2, csem2, multiply_out, nothing)
    out[...] = acc2[...].astype(jnp.bfloat16)

    @pl.loop(1, plane)
    def _(o):
        plane_copy(o).wait_send()

    @pl.loop(1, ring)
    def _(o):
        ring_copy(o).wait_send()

    drain1()
    drain2()
    drain3()
    drain4()


def shards(fsdp, ctx, activations, norm_gain, w_in, w_short, long_filter, skip_gain, w_out):
    rows, tokens = activations.shape
    long_len = long_filter.shape[1]
    plan = Plan(fsdp, ctx, rows, tokens, long_len)
    groups = rows // ROWS
    features = fsdp * rows
    bf16, f32 = jnp.bfloat16, jnp.float32
    dma = pltpu.SemaphoreType.DMA
    anywhere = pl.BlockSpec(memory_space=pl.ANY)
    here = pl.BlockSpec(memory_space=pltpu.VMEM)
    gather_sems = [
        dma((2, max(plan.line, 2))),
        dma((2, 2, plan.half, plan.line)),
        dma((2, 2 * plan.half + 1, plan.line)),
    ]
    scratch = [
        pltpu.VMEM((fsdp, rows, tokens), bf16),
        pltpu.VMEM((fsdp, rows, tokens), bf16),
        pltpu.VMEM((3, rows, features), bf16),
        pltpu.VMEM((rows, features), bf16),
        pltpu.VMEM((rows, tokens), bf16),
        pltpu.VMEM((ROWS, long_len), bf16),
        pltpu.VMEM((ROWS * plan.blocks, LANES), f32),
        pltpu.VMEM((ROWS * plan.blocks, LANES, LANES), bf16),
        pltpu.VMEM((3 * rows, tokens), f32),
        pltpu.VMEM((rows, tokens), f32),
        pltpu.VMEM((plan.plane, ROWS, LANES), f32),
        pltpu.VMEM((plan.ring, ROWS, LANES), f32),
        pltpu.VMEM((ctx, 3, ROWS, tokens), bf16),
        pltpu.VMEM((ctx, 3, ROWS, tokens), bf16),
        pltpu.VMEM((ctx, ROWS, tokens), bf16),
        pltpu.VMEM((ctx, ROWS, tokens), bf16),
        pltpu.VMEM((3, ROWS, LANES + long_len), f32),
        pltpu.VMEM((ROWS * 2 * plan.blocks, LANES), f32),
        pltpu.VMEM((ROWS * plan.blocks, LANES), f32),
        pltpu.VMEM((rows, LANES), f32),
        dma((4,)),
        dma((2, plan.plane)),
        dma((2, plan.ring)),
        *gather_sems,
        *gather_sems,
        dma((2, ctx)),
        dma((2, ctx)),
    ]
    return pl.pallas_call(
        functools.partial(kernel, plan),
        out_shape=jax.ShapeDtypeStruct((rows, tokens), bf16),
        in_specs=[anywhere, here, anywhere, here, anywhere, here, anywhere],
        out_specs=here,
        scratch_shapes=scratch,
        compiler_params=pltpu.CompilerParams(
            collective_id=0, has_side_effects=True, vmem_limit_bytes=56 * 1024 * 1024
        ),
        name="mixer",
    )(
        activations,
        norm_gain.reshape(1, rows),
        w_in,
        w_short.reshape(3, groups, ROWS, w_short.shape[2]),
        long_filter.reshape(groups, ROWS, long_len),
        skip_gain.reshape(1, rows),
        w_out,
    )


def solution(mesh):
    placed = (
        P("fsdp", "ctx"),
        P("fsdp"),
        P(None, "fsdp", None),
        P(None, "fsdp", None),
        P("fsdp", None),
        P("fsdp"),
        P("fsdp", None),
    )
    body = functools.partial(shards, mesh.shape["fsdp"], mesh.shape["ctx"])
    return jax.shard_map(body, mesh=mesh, in_specs=placed, out_specs=P("fsdp", "ctx"), check_vma=False)
```

time: 510 us -> 117 us (0.23)
  waiting for transfers between devices: 196 us -> 0 us
  blocking collectives: 143 us -> 0 us
  Pallas kernels: 0 us -> 114 us
  starting transfers between devices: 86.1 us -> 0 us
  matrix products: 26.3 us -> 0 us
  other arithmetic: 23.3 us -> 0 us
  between operations: 14.3 us -> 0.01 us
  local copies, waits for them, and re-layouts: 15.4 us -> 2.95 us
    all_gather x2 -> x0, waiting for transfers between devices: 184 us -> none  [the longest x1 184 us: shards(): lax.all_gather(mixed, 'fsdp', axis=0, tiled=True)]
    unnamed x1 -> x0, blocking collectives: 143 us -> none
    pallas_call x0 -> x1, Pallas kernels: none -> 114 us  [shards(): pl.pallas_call(functools.partial(kernel, plan), out_shape=jax.ShapeDtypeS...]
    ppermute x8 -> x0, starting transfers between devices: 86.1 us -> none  [shifted(): return lax.ppermute(block, axis, route)]
    dot_general x12 -> x0, matrix products: 26.3 us -> none  [the longest x8 12 us: add_portion(): jnp.einsum('grs,si->gri', block_list, forward_pass, precision=highest_pre...]
    ppermute x8 -> x0, waiting for transfers between devices: 11.5 us -> none  [shifted(): return lax.ppermute(block, axis, route)]
    sub x5 -> x0, other arithmetic: 9.01 us -> none  [complex_product(): left_re * right_re - left_im * right_im]
    concatenate x1 -> x0, local copies, waits for them, and re-layouts: 6.13 us -> none  [shards(): jnp.concatenate([jnp.zeros((channels, local_blocks, filter_spec.shape[2])...]
  transfers between devices with their start and end apart: 10 -> 0, of which waited for: 8 -> 0; matrix products, arithmetic and copies ran while one was open for 4% -> 0% of each run, Pallas kernels for 0% -> 0%
where the time goes in v1:
time: 117 us
  Pallas kernels  114 us (97%)
  local copies, waits for them, and re-layouts  2.95 us (3%)
    pallas_call x1, Pallas kernels, shards(): pl.pallas_call(functools.partial(kernel, plan), out_shape=jax.ShapeDtypeS...  114 us
    unnamed x2, local copies, waits for them, and re-layouts  2.95 us

profile of v1, /device:TPU:1, one launch (start us, length us, event | category | flops | bytes accessed | tf_op | source)
XLA Modules:
  0.0 117.0 jit_solution(6520033189529073309)
XLA Ops:
  0.0 1.4 %copy.8 = f32[3,64,3]{2,1,0:T(8,128)} copy(f32[3,64,3]{1,2,0:T(4,128)} %param.10) | data formatting | bytes 4608 | tf_op args[3]
  1.4 114.0 %mixer.1 = bf16[64,640]{1,0:T(8,128)(2,1)} custom-call(bf16[64,640]{1,0:T(8,128)(2,1)} %act.1, f32[1,64]{1,0:T(1,128)} %bitcast.6, bf16[3,64,4096]{2,1,0:T(8,128)(2,1)} %w_in.1, f32[3,8,8,3]{3,2,1,0:T(8,128)} %bitcast.5, bf16[8,8,5120]{2,1,0:T(8,128)(2,1)} %bitcast.4, f32[1,64]{1,0:T(1,128)} %bitcast.7, bf16[64,4096]{1,0:T(8,128)(2,1)} %w_out.1), custom_call_target="tpu_custom_call" | custom-call | tf_op jit(solution)/shard_map/mixer/pallas_call | solution.py:385
  115.5 1.5 %copy.10 = bf16[64,640]{1,0:T(8,128)(2,1)} copy(bf16[64,640]{1,0:T(8,128)(2,1)} %mixer.1) | data formatting | bytes 163840

commit v2 on v1

--- a/solution.py
+++ b/solution.py
@@ -35,8 +35,8 @@
 def kernel(
     plan, act, gain, w_in, w_short, filt, skip, w_out, out,
     gath, mixg, win, wout, xin, hin, hrow, tmat, acc, acc2, plane_sum, ring_sum,
-    pbuf, rbuf, mbuf, mrecv, seq, gseq, fseq, skipb,
-    lsem, plane_sem, ring_sem, zsem, ysem, csem, zsem2, ysem2, csem2, asem, bsem,
+    pbuf, rbuf, mbuf, mrecv, seq, gseq, fseq, skipb, tapb,
+    lsem, plane_sem, ring_sem, zsem, ysem, lastsem, csem, zsem2, ysem2, lastsem2, csem2, asem, bsem,
 ):
     me = lax.axis_index("fsdp")
     ctx = lax.axis_index("ctx")
@@ -93,6 +93,8 @@
     for k in range(plan.token_tiles):
         plane_sum[0, k : k + 1, :] = squares[:, k * LANES : (k + 1) * LANES]
     skipb[...] = jnp.broadcast_to(column(skip[...]), (rows, LANES))
+    for k in range(9):
+        tapb[k] = jnp.broadcast_to(column(w_short[k // 3, k % 3 : k % 3 + 1, :]), (rows, LANES))
     acc[...] = jnp.zeros_like(acc)
     acc2[...] = jnp.zeros_like(acc2)
     gseq[...] = jnp.zeros_like(gseq)
@@ -109,82 +111,121 @@
             ring_sum.at[0], ring_sum.at[o], ring_sem.at[0, o], ring_sem.at[1, o], {"fsdp": turn(y + o) * plane + p}
         )
 
-    def gather(buf, zs, ys, cs, multiply, fillers):
+    def gather(buf, zs, ys, bs, cs, multiply, fillers):
+        first = rows - rows // 4
+        last = ring - 1
+
+        def place(r):
+            if r < half:
+                return turn(y - r)
+            return turn(y + (r - half + 1)) if r < last else turn(y + half)
+
+        def columns(s):
+            return [s, half - 1 + s] if s < half else [last]
+
         def zcopy(o, zz_from):
-            block = buf.at[at(y, zz_from, core)]
-            return copy_to(block, block, zs.at[0, o], zs.at[1, o], {"fsdp": at(y, z ^ o, core)})
-
-        def origin(d, s):
-            return turn(y - s) if d == 0 else turn(y + s)
-
-        def part(block, d, s):
+            view = buf.at[at(y, zz_from, core), pl.ds(0, first)]
+            return copy_to(view, view, zs.at[0, o], zs.at[1, o], {"fsdp": at(y, z ^ o, core)})
+
+        def ycopy(r, o, yy, step, whole):
+            block = at(yy, z ^ o, core)
+            view = buf.at[block] if whole else buf.at[block, pl.ds(0, first)]
+            return copy_to(view, view, ys.at[0, r, o], ys.at[1, r, o], {"fsdp": at(turn(y + step), z, core)})
+
+        def bcopy(r, o, zz_from):
+            view = buf.at[at(place(r), zz_from, core), pl.ds(first, rows - first)]
+            return copy_to(view, view, bs.at[0, r, o], bs.at[1, r, o], {"fsdp": at(y, z ^ o, core)})
+
+        def ccopy(r, o, cc):
+            block = buf.at[at(place(r), z ^ o, cc)]
+            return copy_to(block, block, cs.at[0, r, o], cs.at[1, r, o], {"fsdp": at(y, z, 1 - core)})
+
+        def pass_on(d, s, o, whole):
+            yy = turn(y - (s - 1)) if d == 0 else turn(y + (s - 1))
+            copy = ycopy(columns(s)[d if s < half else 0], o, yy, 1 - 2 * d, whole)
             if s < half:
-                return buf.at[block]
-            return buf.at[block, pl.ds(d * (rows // 2), rows // 2)]
-
-        def ycopy(d, s, o, receive):
-            came = s if receive else s - 1
-            block = at(origin(d, came), z ^ o, core)
-            view = part(block, d, s)
-            to = turn(y + 1) if d == 0 else turn(y - 1)
-            return copy_to(view, view, ys.at[0, d, s - 1, o], ys.at[1, d, s - 1, o], {"fsdp": at(to, z, core)})
-
-        def ccopy(d, s, o, mine):
-            r = s + d * half
-            block = at(origin(d, s), z ^ o, core if mine else 1 - core)
-            view = part(block, d, s)
-            return copy_to(view, view, cs.at[0, r, o], cs.at[1, r, o], {"fsdp": at(y, z, 1 - core)})
-
+                copy.start()
+            else:
+                pl.when(core == d)(copy.start)
+
+        def arrive(s, o):
+            for d, r in enumerate(columns(s)):
+                ycopy(r, o, place(r), 1, o == 0).wait_recv()
+                if s < half:
+                    pass_on(d, s + 1, o, o == 0)
+                if o == 0:
+                    spread_line(r)
+
+        def spread_line(r):
+            for k in range(1, line):
+                bcopy(r, k, z).start()
+            if r:
+                ccopy(r, 0, core).start()
+
+        def arrive_line(o):
+            zcopy(o, z ^ o).wait_recv()
+            for d in range(2):
+                pass_on(d, 1, o, False)
+            if o == 1:
+                spread_line(0)
+
+        def hand_over(s):
+            for r in columns(s) if s else [0]:
+                @pl.loop(1, line)
+                def _(o):
+                    bcopy(r, o, z ^ o).wait_recv()
+                    ccopy(r, o, core).start()
+
+        def finish(s):
+            for r in columns(s) if s else [0]:
+                @pl.loop(0, line)
+                def _(o):
+                    ccopy(r, o, 1 - core).wait_recv()
+
+                multiply(place(r))
+
+        def drain(s):
+            for r in columns(s) if s else [0]:
+                if s:
+                    ycopy(r, 0, y, 1, True).wait_send()
+                ccopy(r, 0, core).wait_send()
+
+                @pl.loop(1, line)
+                def _(o):
+                    if s:
+                        ycopy(r, o, y, 1, False).wait_send()
+                    else:
+                        zcopy(o, z).wait_send()
+                    bcopy(r, o, z).wait_send()
+                    ccopy(r, o, core).wait_send()
+
+        for d in range(2):
+            pass_on(d, 1, 0, True)
         for o in range(1, line):
             zcopy(o, z).start()
-        for d in range(2):
-            ycopy(d, 1, 0, False).start()
-        ccopy(0, 0, 0, True).start()
-        fillers[0]()
+        ccopy(0, 0, core).start()
+
+        hop = 4.8
+        crossed = [0.0] + [2.0 + 2.2 * o for o in range(1, line)]
+        events = list(fillers)
         for o in range(1, line):
-            zcopy(o, z ^ o).wait_recv()
-            for d in range(2):
-                ycopy(d, 1, o, False).start()
-            ccopy(0, 0, o, True).start()
-        fillers[1]()
-        for s in range(1, half + 1):
-            @pl.loop(0, line)
-            def _(o):
-                for d in range(2):
-                    ycopy(d, s, o, True).wait_recv()
-                    if s < half:
-                        ycopy(d, s + 1, o, False).start()
-                    ccopy(d, s, o, True).start()
-
-            @pl.loop(0, line)
-            def _(o):
-                for d in range(2 if s > 1 else 1):
-                    ccopy(d, s - 1, o, False).wait_recv()
-
-            for d in range(2 if s > 1 else 1):
-                multiply(origin(d, s - 1))
-            fillers[1 + s]()
-
-        @pl.loop(0, line)
-        def _(o):
-            for d in range(2):
-                ccopy(d, half, o, False).wait_recv()
-
-        multiply(origin(0, half))
-
-        def drain():
-            for o in range(1, line):
-                zcopy(o, z).wait_send()
-
-            @pl.loop(0, line)
-            def _(o):
-                ccopy(0, 0, o, True).wait_send()
-                for s in range(1, half + 1):
-                    for d in range(2):
-                        ycopy(d, s, o, False).wait_send()
-                        ccopy(d, s, o, True).wait_send()
-
-        return drain
+            events.append((crossed[o], functools.partial(arrive_line, o)))
+        for s in range(half + 1):
+            for o in range(line if s else 0):
+                events.append((crossed[o] + hop * s, functools.partial(arrive, s, o)))
+            handed = max(crossed[-1] + hop * s, hop * (s + 1)) + 0.1
+            events.append((handed, functools.partial(hand_over, s)))
+            events.append((handed + 2.0, functools.partial(finish, s)))
+            if s < half - 1:
+                events.append((handed + 10.0, functools.partial(drain, s)))
+        for _, event in sorted(events, key=lambda e: e[0]):
+            event()
+
+        def rest():
+            drain(half - 1)
+            drain(half)
+
+        return rest
 
     width = plane * rows
 
@@ -217,15 +258,13 @@
                 tmat[r] = jnp.where(later, rolled, before).astype(jnp.bfloat16)
                 return rolled
 
-            lax.fori_loop(0, plan.blocks, body, jnp.zeros((LANES, LANES), jnp.float32))
+            lax.fori_loop(0, plan.blocks, body, jnp.zeros((LANES, LANES), jnp.float32), unroll=min(8, plan.blocks))
 
     def start_plane():
         @pl.loop(1, plane)
         def _(o):
             plane_copy(o).start()
 
-        spread_filter()
-
     def start_ring():
         @pl.loop(1, plane)
         def _(o):
@@ -237,10 +276,9 @@
         def _(o):
             ring_copy(o).start()
 
-        band(0, 2)
-
-    bands = [functools.partial(band, 2 + 6 * i // half, 2 + 6 * (i + 1) // half) for i in range(half)]
-    drain1 = gather(gath, zsem, ysem, csem, multiply_in, [start_plane, start_ring] + bands)
+    fillers = [(0.0, start_plane), (4.3, spread_filter), (8.3, start_ring)]
+    fillers += [(7.0 + 1.9 * i, functools.partial(band, i, i + 1)) for i in range(ROWS)]
+    drain1 = gather(gath, zsem, ysem, lastsem, csem, multiply_in, fillers)
 
     @pl.loop(1, ring)
     def _(o):
@@ -256,7 +294,7 @@
                 n = rows // plan.ctx
                 pbuf[j, s, :, lanes] = scaled[j * n : (j + 1) * n].astype(jnp.bfloat16)
 
-    def swap(src, dst, sem):
+    def swap(src, dst, sem, meanwhile):
         def one(o):
             return copy_to(src.at[ctx ^ o], dst.at[ctx], sem.at[0, o], sem.at[1, o], {"ctx": ctx ^ o})
 
@@ -269,6 +307,7 @@
                 one(o).start()
 
         dst[ctx] = src[ctx]
+        meanwhile()
         if plan.ctx > 1:
             @pl.loop(1, plan.ctx)
             def _(o):
@@ -282,17 +321,28 @@
 
         return drain
 
-    drain2 = swap(pbuf, rbuf, asem)
+    def drain_first():
+        @pl.loop(1, plane)
+        def _(o):
+            plane_copy(o).wait_send()
+
+        @pl.loop(1, ring)
+        def _(o):
+            ring_copy(o).wait_send()
+
+        drain1()
+
+    drain2 = swap(pbuf, rbuf, asem, drain_first)
 
     for j in range(plan.ctx):
         for s in range(3):
             seq[s, :, LANES + j * tokens : LANES + (j + 1) * tokens] = rbuf[j, s].astype(jnp.float32)
 
     def smooth(s):
-        taps = w_short[s, ctx]
+        taps = [tapb[3 * s + k, pl.ds(ctx * ROWS, ROWS), :][:, 0:1] for k in range(3)]
         full = seq[s]
-        total = taps[:, 0:1] * full + taps[:, 1:2] * pltpu.roll(full, 1, 1)
-        total = total + taps[:, 2:3] * pltpu.roll(full, 2, 1)
+        total = taps[0] * full + taps[1] * pltpu.roll(full, 1, 1)
+        total = total + taps[2] * pltpu.roll(full, 2, 1)
         return total[:, LANES:]
 
     gated = (smooth(1) * smooth(2)).astype(jnp.bfloat16).astype(jnp.float32)
@@ -317,23 +367,11 @@
         j, k = b // plan.token_tiles, b % plan.token_tiles
         mbuf[j, :, k * LANES : (k + 1) * LANES] = value.astype(jnp.bfloat16)
 
-    drain3 = swap(mbuf, mrecv, bsem)
+    drain3 = swap(mbuf, mrecv, bsem, drain2)
     mixg[me] = mrecv[...].astype(jnp.float32).reshape(rows, tokens).astype(jnp.bfloat16)
 
-    nothing = [lambda: None] * (half + 2)
-    drain4 = gather(mixg, zsem2, ysem2, csem2, multiply_out, nothing)
+    drain4 = gather(mixg, zsem2, ysem2, lastsem2, csem2, multiply_out, [])
     out[...] = acc2[...].astype(jnp.bfloat16)
-
-    @pl.loop(1, plane)
-    def _(o):
-        plane_copy(o).wait_send()
-
-    @pl.loop(1, ring)
-    def _(o):
-        ring_copy(o).wait_send()
-
-    drain1()
-    drain2()
     drain3()
     drain4()
 
@@ -350,8 +388,9 @@
     here = pl.BlockSpec(memory_space=pltpu.VMEM)
     gather_sems = [
         dma((2, max(plan.line, 2))),
-        dma((2, 2, plan.half, plan.line)),
-        dma((2, 2 * plan.half + 1, plan.line)),
+        dma((2, plan.ring, plan.line)),
+        dma((2, plan.ring, max(plan.line, 2))),
+        dma((2, plan.ring, plan.line)),
     ]
     scratch = [
         pltpu.VMEM((fsdp, rows, tokens), bf16),
@@ -374,6 +413,7 @@
         pltpu.VMEM((ROWS * 2 * plan.blocks, LANES), f32),
         pltpu.VMEM((ROWS * plan.blocks, LANES), f32),
         pltpu.VMEM((rows, LANES), f32),
+        pltpu.VMEM((9, rows, LANES), f32),
         dma((4,)),
         dma((2, plan.plane)),
         dma((2, plan.ring)),
@@ -396,7 +436,7 @@
         activations,
         norm_gain.reshape(1, rows),
         w_in,
-        w_short.reshape(3, groups, ROWS, w_short.shape[2]),
+        jnp.transpose(w_short, (0, 2, 1)),
         long_filter.reshape(groups, ROWS, long_len),
         skip_gain.reshape(1, rows),
         w_out,

time: 117 us -> 102 us (0.87)
  Pallas kernels: 114 us -> 100 us
  local copies, waits for them, and re-layouts: 2.95 us -> 1.53 us
    pallas_call x1, Pallas kernels: 114 us -> 100 us  [shards(): pl.pallas_call(functools.partial(kernel, plan), out_shape=jax.ShapeDtypeS...]
    unnamed x2 -> x1, local copies, waits for them, and re-layouts: 2.95 us -> 1.53 us
where the time goes in v2:
time: 102 us
  Pallas kernels  100 us (98%)
  local copies, waits for them, and re-layouts  1.53 us (2%)
    pallas_call x1, Pallas kernels, shards(): pl.pallas_call(functools.partial(kernel, plan), out_shape=jax.ShapeDtypeS...  100 us

profile of v2, /device:TPU:1, one launch (start us, length us, event | category | flops | bytes accessed | tf_op | source)
XLA Modules:
  0.0 102.0 jit_solution(14443065302300112596)
XLA Ops:
  0.0 100.5 %mixer.1 = bf16[64,640]{1,0:T(8,128)(2,1)} custom-call(bf16[64,640]{1,0:T(8,128)(2,1)} %act.1, f32[1,64]{1,0:T(1,128)} %bitcast.6, bf16[3,64,4096]{2,1,0:T(8,128)(2,1)} %w_in.1, f32[3,3,64]{2,1,0:T(4,128)} %bitcast.5, bf16[8,8,5120]{2,1,0:T(8,128)(2,1)} %bitcast.4, f32[1,64]{1,0:T(1,128)} %bitcast.7, bf16[64,4096]{1,0:T(8,128)(2,1)} %w_out.1), custom_call_target="tpu_custom_call" | custom-call | tf_op jit(solution)/shard_map/mixer/pallas_call | solution.py:425
  100.5 1.5 %copy.9 = bf16[64,640]{1,0:T(8,128)(2,1)} copy(bf16[64,640]{1,0:T(8,128)(2,1)} %mixer.1) | data formatting | bytes 163840

commit v3 on v2

--- a/solution.py
+++ b/solution.py
@@ -35,8 +35,8 @@
 def kernel(
     plan, act, gain, w_in, w_short, filt, skip, w_out, out,
     gath, mixg, win, wout, xin, hin, hrow, tmat, acc, acc2, plane_sum, ring_sum,
-    pbuf, rbuf, mbuf, mrecv, seq, gseq, fseq, skipb, tapb,
-    lsem, plane_sem, ring_sem, zsem, ysem, lastsem, csem, zsem2, ysem2, lastsem2, csem2, asem, bsem,
+    pbuf, rbuf, qbuf, qrecv, mbuf, mrecv, seq, gseq, fseq, skipb, tapb,
+    lsem, plane_sem, ring_sem, zsem, ysem, lastsem, csem, zsem2, ysem2, lastsem2, csem2, asem, qsem, bsem,
 ):
     me = lax.axis_index("fsdp")
     ctx = lax.axis_index("ctx")
@@ -169,12 +169,10 @@
             if o == 1:
                 spread_line(0)
 
-        def hand_over(s):
+        def hand_over(s, o):
             for r in columns(s) if s else [0]:
-                @pl.loop(1, line)
-                def _(o):
-                    bcopy(r, o, z ^ o).wait_recv()
-                    ccopy(r, o, core).start()
+                bcopy(r, o, z ^ o).wait_recv()
+                ccopy(r, o, core).start()
 
         def finish(s):
             for r in columns(s) if s else [0]:
@@ -205,7 +203,7 @@
             zcopy(o, z).start()
         ccopy(0, 0, core).start()
 
-        hop = 4.8
+        hop = 5.6
         crossed = [0.0] + [2.0 + 2.2 * o for o in range(1, line)]
         events = list(fillers)
         for o in range(1, line):
@@ -213,8 +211,10 @@
         for s in range(half + 1):
             for o in range(line if s else 0):
                 events.append((crossed[o] + hop * s, functools.partial(arrive, s, o)))
+            for o in range(1, line):
+                handed = max(crossed[o] + hop * s, hop * (s + 1)) + 0.1
+                events.append((handed, functools.partial(hand_over, s, o)))
             handed = max(crossed[-1] + hop * s, hop * (s + 1)) + 0.1
-            events.append((handed, functools.partial(hand_over, s)))
             events.append((handed + 2.0, functools.partial(finish, s)))
             if s < half - 1:
                 events.append((handed + 10.0, functools.partial(drain, s)))
@@ -286,57 +286,63 @@
 
     features = plan.fsdp * rows
     factor = lax.rsqrt(jnp.sum(ring_sum[...], axis=0) / features + EPSILON)
-    for k in range(plan.token_tiles):
-        lanes = slice(k * LANES, (k + 1) * LANES)
-        for s in range(3):
+
+    def project(s, store):
+        for k in range(plan.token_tiles):
+            lanes = slice(k * LANES, (k + 1) * LANES)
             scaled = acc[s * rows : (s + 1) * rows, lanes] * factor[k : k + 1, :]
             for j in range(plan.ctx):
-                n = rows // plan.ctx
-                pbuf[j, s, :, lanes] = scaled[j * n : (j + 1) * n].astype(jnp.bfloat16)
-
-    def swap(src, dst, sem, meanwhile):
-        def one(o):
-            return copy_to(src.at[ctx ^ o], dst.at[ctx], sem.at[0, o], sem.at[1, o], {"ctx": ctx ^ o})
-
-        def arrival(o):
-            return copy_to(src.at[ctx ^ o], dst.at[ctx ^ o], sem.at[0, o], sem.at[1, o], {"ctx": ctx ^ o})
-
-        if plan.ctx > 1:
-            @pl.loop(1, plan.ctx)
-            def _(o):
-                one(o).start()
-
+                store(j, lanes, scaled[j * ROWS : (j + 1) * ROWS].astype(jnp.bfloat16))
+
+    def keep_key(j, lanes, value):
+        pbuf[j, 0, :, lanes] = value
+
+    def keep_value(j, lanes, value):
+        pbuf[j, 1, :, lanes] = value
+
+    def keep_query(j, lanes, value):
+        qbuf[j, :, lanes] = value
+
+    def swap(src, dst, sem):
+        order = [o for o in range(1, plan.ctx) if o % 2] + [o for o in range(2, plan.ctx, 2)]
+
+        def copy(o, slot):
+            return copy_to(src.at[ctx ^ o], dst.at[slot], sem.at[0, o], sem.at[1, o], {"ctx": ctx ^ o})
+
+        for o in order:
+            copy(o, ctx).start()
         dst[ctx] = src[ctx]
-        meanwhile()
-        if plan.ctx > 1:
-            @pl.loop(1, plan.ctx)
-            def _(o):
-                arrival(o).wait_recv()
+
+        def arrive():
+            for o in order:
+                copy(o, ctx ^ o).wait_recv()
 
         def drain():
-            if plan.ctx > 1:
-                @pl.loop(1, plan.ctx)
-                def _(o):
-                    one(o).wait_send()
-
-        return drain
-
-    def drain_first():
-        @pl.loop(1, plane)
-        def _(o):
-            plane_copy(o).wait_send()
-
-        @pl.loop(1, ring)
-        def _(o):
-            ring_copy(o).wait_send()
-
-        drain1()
-
-    drain2 = swap(pbuf, rbuf, asem, drain_first)
+            for o in order:
+                copy(o, ctx).wait_send()
+
+        return arrive, drain
+
+    project(1, keep_key)
+    project(2, keep_value)
+    arrive_gate, drain_gate = swap(pbuf, rbuf, asem)
+    project(0, keep_query)
+    arrive_query, drain_query = swap(qbuf, qrecv, qsem)
+
+    @pl.loop(1, plane)
+    def _(o):
+        plane_copy(o).wait_send()
+
+    @pl.loop(1, ring)
+    def _(o):
+        ring_copy(o).wait_send()
+
+    drain1()
+    arrive_gate()
 
     for j in range(plan.ctx):
-        for s in range(3):
-            seq[s, :, LANES + j * tokens : LANES + (j + 1) * tokens] = rbuf[j, s].astype(jnp.float32)
+        for s in range(2):
+            seq[s + 1, :, LANES + j * tokens : LANES + (j + 1) * tokens] = rbuf[j, s].astype(jnp.float32)
 
     def smooth(s):
         taps = [tapb[3 * s + k, pl.ds(ctx * ROWS, ROWS), :][:, 0:1] for k in range(3)]
@@ -346,7 +352,6 @@
         return total[:, LANES:]
 
     gated = (smooth(1) * smooth(2)).astype(jnp.bfloat16).astype(jnp.float32)
-    query = smooth(0)
     blocks = plan.blocks
     for b in range(blocks):
         gseq[pl.ds(blocks + b, ROWS, stride=2 * blocks), :] = gated[:, b * LANES : (b + 1) * LANES]
@@ -360,6 +365,10 @@
         rhs = tmat[pl.ds(c * blocks, blocks)].reshape(blocks * LANES, LANES)
         fseq[pl.ds(c * blocks, blocks), :] = jnp.dot(lhs, rhs, preferred_element_type=jnp.float32)
 
+    arrive_query()
+    for j in range(plan.ctx):
+        seq[0, :, LANES + j * tokens : LANES + (j + 1) * tokens] = qrecv[j].astype(jnp.float32)
+    query = smooth(0)
     direct = skipb[pl.ds(ctx * ROWS, ROWS), :]
     for b in range(blocks):
         lanes = slice(b * LANES, (b + 1) * LANES)
@@ -367,12 +376,15 @@
         j, k = b // plan.token_tiles, b % plan.token_tiles
         mbuf[j, :, k * LANES : (k + 1) * LANES] = value.astype(jnp.bfloat16)
 
-    drain3 = swap(mbuf, mrecv, bsem, drain2)
+    arrive_mixed, drain_mixed = swap(mbuf, mrecv, bsem)
+    drain_gate()
+    drain_query()
+    arrive_mixed()
     mixg[me] = mrecv[...].astype(jnp.float32).reshape(rows, tokens).astype(jnp.bfloat16)
 
     drain4 = gather(mixg, zsem2, ysem2, lastsem2, csem2, multiply_out, [])
     out[...] = acc2[...].astype(jnp.bfloat16)
-    drain3()
+    drain_mixed()
     drain4()
 
 
@@ -405,8 +417,10 @@
         pltpu.VMEM((rows, tokens), f32),
         pltpu.VMEM((plan.plane, ROWS, LANES), f32),
         pltpu.VMEM((plan.ring, ROWS, LANES), f32),
-        pltpu.VMEM((ctx, 3, ROWS, tokens), bf16),
-        pltpu.VMEM((ctx, 3, ROWS, tokens), bf16),
+        pltpu.VMEM((ctx, 2, ROWS, tokens), bf16),
+        pltpu.VMEM((ctx, 2, ROWS, tokens), bf16),
+        pltpu.VMEM((ctx, ROWS, tokens), bf16),
+        pltpu.VMEM((ctx, ROWS, tokens), bf16),
         pltpu.VMEM((ctx, ROWS, tokens), bf16),
         pltpu.VMEM((ctx, ROWS, tokens), bf16),
         pltpu.VMEM((3, ROWS, LANES + long_len), f32),
@@ -419,6 +433,7 @@
         dma((2, plan.ring)),
         *gather_sems,
         *gather_sems,
+        dma((2, ctx)),
         dma((2, ctx)),
         dma((2, ctx)),
     ]

time: 102 us -> 98.9 us (0.970)
  Pallas kernels: 100 us -> 97.2 us
    pallas_call x1, Pallas kernels: 100 us -> 97.2 us  [shards(): pl.pallas_call(functools.partial(kernel, plan), out_shape=jax.ShapeDtypeS...]
where the time goes in v3:
time: 98.9 us; the launch traced here: 98.7 us
  Pallas kernels  97.2 us (98%)
  local copies, waits for them, and re-layouts  1.53 us (2%)
    pallas_call x1, Pallas kernels, shards(): pl.pallas_call(functools.partial(kernel, plan), out_shape=jax.ShapeDtypeS...  97.2 us

profile of v3, /device:TPU:1, one launch (start us, length us, event | category | flops | bytes accessed | tf_op | source)
XLA Modules:
  0.0 98.7 jit_solution(5159070073659749795)
XLA Ops:
  0.0 97.2 %mixer.1 = bf16[64,640]{1,0:T(8,128)(2,1)} custom-call(bf16[64,640]{1,0:T(8,128)(2,1)} %act.1, f32[1,64]{1,0:T(1,128)} %bitcast.6, bf16[3,64,4096]{2,1,0:T(8,128)(2,1)} %w_in.1, f32[3,3,64]{2,1,0:T(4,128)} %bitcast.5, bf16[8,8,5120]{2,1,0:T(8,128)(2,1)} %bitcast.4, f32[1,64]{1,0:T(1,128)} %bitcast.7, bf16[64,4096]{1,0:T(8,128)(2,1)} %w_out.1), custom_call_target="tpu_custom_call" | custom-call | tf_op jit(solution)/shard_map/mixer/pallas_call | solution.py:440
  97.2 1.5 %copy.9 = bf16[64,640]{1,0:T(8,128)(2,1)} copy(bf16[64,640]{1,0:T(8,128)(2,1)} %mixer.1) | data formatting | bytes 163840

commit v4 on v3

--- a/solution.py
+++ b/solution.py
@@ -34,7 +34,7 @@
 
 def kernel(
     plan, act, gain, w_in, w_short, filt, skip, w_out, out,
-    gath, mixg, win, wout, xin, hin, hrow, tmat, acc, acc2, plane_sum, ring_sum,
+    gath, mixg, win, wout, xin, hin, hrow, tmat, acc, acc2, plane_sum, ring_sum, scale,
     pbuf, rbuf, qbuf, qrecv, mbuf, mrecv, seq, gseq, fseq, skipb, tapb,
     lsem, plane_sem, ring_sem, zsem, ysem, lastsem, csem, zsem2, ysem2, lastsem2, csem2, asem, qsem, bsem,
 ):
@@ -59,26 +59,25 @@
         pltpu.make_async_copy(w_in, win, lsem.at[2]),
         pltpu.make_async_copy(w_out, wout, lsem.at[3]),
     ]
-    for load in loads:
-        load.start()
-
+    loads[0].start()
     barrier = pltpu.get_barrier_semaphore()
 
     def greet(device):
         pl.semaphore_signal(barrier, inc=1, device_id=device, device_id_type=MESH)
+
+    for o in [o for o in range(1, plan.ctx) if o % 2] + [o for o in range(2, plan.ctx, 2)]:
+        greet({"ctx": ctx ^ o})
+
+    @pl.loop(1, ring)
+    def _(o):
+        greet({"fsdp": turn(y + o) * plane + p})
 
     @pl.loop(1, plane)
     def _(o):
         greet({"fsdp": y * plane + (p ^ o)})
 
-    @pl.loop(1, ring)
-    def _(o):
-        greet({"fsdp": turn(y + o) * plane + p})
-
-    if plan.ctx > 1:
-        @pl.loop(1, plan.ctx)
-        def _(o):
-            greet({"ctx": ctx ^ o})
+    for load in loads[1:]:
+        load.start()
 
     def column(row):
         n = row.shape[1]
@@ -216,16 +215,14 @@
                 events.append((handed, functools.partial(hand_over, s, o)))
             handed = max(crossed[-1] + hop * s, hop * (s + 1)) + 0.1
             events.append((handed + 2.0, functools.partial(finish, s)))
-            if s < half - 1:
+            if s == half:
+                events.append((handed + 1.0, functools.partial(drain, s - 1)))
+            elif s < half - 1:
                 events.append((handed + 10.0, functools.partial(drain, s)))
         for _, event in sorted(events, key=lambda e: e[0]):
             event()
 
-        def rest():
-            drain(half - 1)
-            drain(half)
-
-        return rest
+        return functools.partial(drain, half)
 
     width = plane * rows
 
@@ -276,16 +273,18 @@
         def _(o):
             ring_copy(o).start()
 
-    fillers = [(0.0, start_plane), (4.3, spread_filter), (8.3, start_ring)]
+    def end_sum():
+        @pl.loop(1, ring)
+        def _(o):
+            ring_copy(o).wait_recv()
+
+        scale[...] = lax.rsqrt(jnp.sum(ring_sum[...], axis=0) / (plan.fsdp * rows) + EPSILON)
+
+    fillers = [(21.0, end_sum), (0.0, start_plane), (4.3, spread_filter), (8.3, start_ring)]
     fillers += [(7.0 + 1.9 * i, functools.partial(band, i, i + 1)) for i in range(ROWS)]
     drain1 = gather(gath, zsem, ysem, lastsem, csem, multiply_in, fillers)
 
-    @pl.loop(1, ring)
-    def _(o):
-        ring_copy(o).wait_recv()
-
-    features = plan.fsdp * rows
-    factor = lax.rsqrt(jnp.sum(ring_sum[...], axis=0) / features + EPSILON)
+    factor = scale[...]
 
     def project(s, store):
         for k in range(plan.token_tiles):
@@ -356,7 +355,7 @@
     for b in range(blocks):
         gseq[pl.ds(blocks + b, ROWS, stride=2 * blocks), :] = gated[:, b * LANES : (b + 1) * LANES]
 
-    @pl.loop(0, ROWS)
+    @pl.loop(0, ROWS, unroll=2)
     def _(c):
         base = c * 2 * blocks + blocks
         lhs = jnp.concatenate(
@@ -417,6 +416,7 @@
         pltpu.VMEM((rows, tokens), f32),
         pltpu.VMEM((plan.plane, ROWS, LANES), f32),
         pltpu.VMEM((plan.ring, ROWS, LANES), f32),
+        pltpu.VMEM((ROWS, LANES), f32),
         pltpu.VMEM((ctx, 2, ROWS, tokens), bf16),
         pltpu.VMEM((ctx, 2, ROWS, tokens), bf16),
         pltpu.VMEM((ctx, ROWS, tokens), bf16),

time: 98.9 us -> 98.3 us (level)
  no operation moved by 1% of the time
where the time goes in v4:
time: 98.3 us; the launch traced here: 98.1 us
  Pallas kernels  96.5 us (98%)
  local copies, waits for them, and re-layouts  1.53 us (2%)
    pallas_call x1, Pallas kernels, shards(): pl.pallas_call(functools.partial(kernel, plan), out_shape=jax.ShapeDtypeS...  96.5 us

profile of v4, /device:TPU:1, one launch (start us, length us, event | category | flops | bytes accessed | tf_op | source)
XLA Modules:
  0.0 98.1 jit_solution(14716098564721050761)
XLA Ops:
  0.0 96.5 %mixer.1 = bf16[64,640]{1,0:T(8,128)(2,1)} custom-call(bf16[64,640]{1,0:T(8,128)(2,1)} %act.1, f32[1,64]{1,0:T(1,128)} %bitcast.6, bf16[3,64,4096]{2,1,0:T(8,128)(2,1)} %w_in.1, f32[3,3,64]{2,1,0:T(4,128)} %bitcast.5, bf16[8,8,5120]{2,1,0:T(8,128)(2,1)} %bitcast.4, f32[1,64]{1,0:T(1,128)} %bitcast.7, bf16[64,4096]{1,0:T(8,128)(2,1)} %w_out.1), custom_call_target="tpu_custom_call" | custom-call | tf_op jit(solution)/shard_map/mixer/pallas_call | solution.py:440
  96.5 1.5 %copy.9 = bf16[64,640]{1,0:T(8,128)(2,1)} copy(bf16[64,640]{1,0:T(8,128)(2,1)} %mixer.1) | data formatting | bytes 163840

commit v5 on v4

--- a/solution.py
+++ b/solution.py
@@ -166,6 +166,8 @@
             for d in range(2):
                 pass_on(d, 1, o, False)
             if o == 1:
+                for k in range(3, line):
+                    zcopy(k, z).start()
                 spread_line(0)
 
         def hand_over(s, o):
@@ -198,7 +200,7 @@
 
         for d in range(2):
             pass_on(d, 1, 0, True)
-        for o in range(1, line):
+        for o in range(1, min(line, 3)):
             zcopy(o, z).start()
         ccopy(0, 0, core).start()
 

time: 98.3 us -> 100 us (1.017)
  Pallas kernels: 96.5 us -> 98.7 us
    pallas_call x1, Pallas kernels: 96.5 us -> 98.7 us  [shards(): pl.pallas_call(functools.partial(kernel, plan), out_shape=jax.ShapeDtypeS...]
where the time goes in v5:
time: 100 us
  Pallas kernels  98.7 us (99%)
  local copies, waits for them, and re-layouts  1.53 us (2%)
    pallas_call x1, Pallas kernels, shards(): pl.pallas_call(functools.partial(kernel, plan), out_shape=jax.ShapeDtypeS...  98.7 us

profile of v5, /device:TPU:1, one launch (start us, length us, event | category | flops | bytes accessed | tf_op | source)
XLA Modules:
  0.0 100.2 jit_solution(16305339863782273682)
XLA Ops:
  0.0 98.7 %mixer.1 = bf16[64,640]{1,0:T(8,128)(2,1)} custom-call(bf16[64,640]{1,0:T(8,128)(2,1)} %act.1, f32[1,64]{1,0:T(1,128)} %bitcast.6, bf16[3,64,4096]{2,1,0:T(8,128)(2,1)} %w_in.1, f32[3,3,64]{2,1,0:T(4,128)} %bitcast.5, bf16[8,8,5120]{2,1,0:T(8,128)(2,1)} %bitcast.4, f32[1,64]{1,0:T(1,128)} %bitcast.7, bf16[64,4096]{1,0:T(8,128)(2,1)} %w_out.1), custom_call_target="tpu_custom_call" | custom-call | tf_op jit(solution)/shard_map/mixer/pallas_call | solution.py:442
  98.7 1.5 %copy.9 = bf16[64,640]{1,0:T(8,128)(2,1)} copy(bf16[64,640]{1,0:T(8,128)(2,1)} %mixer.1) | data formatting | bytes 163840

commit v6 on v4

--- a/solution.py
+++ b/solution.py
@@ -196,10 +196,10 @@
                     bcopy(r, o, z).wait_send()
                     ccopy(r, o, core).wait_send()
 
+        for o in reversed(range(1, line)):
+            zcopy(o, z).start()
         for d in range(2):
             pass_on(d, 1, 0, True)
-        for o in range(1, line):
-            zcopy(o, z).start()
         ccopy(0, 0, core).start()
 
         hop = 5.6

time: 98.3 us -> 99.7 us (1.014)
  Pallas kernels: 96.5 us -> 98 us
    pallas_call x1, Pallas kernels: 96.5 us -> 98 us  [shards(): pl.pallas_call(functools.partial(kernel, plan), out_shape=jax.ShapeDtypeS...]
where the time goes in v6:
time: 99.7 us; the launch traced here: 99.5 us
  Pallas kernels  98 us (98%)
  local copies, waits for them, and re-layouts  1.53 us (2%)
    pallas_call x1, Pallas kernels, shards(): pl.pallas_call(functools.partial(kernel, plan), out_shape=jax.ShapeDtypeS...  98 us

profile of v6, /device:TPU:1, one launch (start us, length us, event | category | flops | bytes accessed | tf_op | source)
XLA Modules:
  0.0 99.5 jit_solution(5162229525769766390)
XLA Ops:
  0.0 98.0 %mixer.1 = bf16[64,640]{1,0:T(8,128)(2,1)} custom-call(bf16[64,640]{1,0:T(8,128)(2,1)} %act.1, f32[1,64]{1,0:T(1,128)} %bitcast.6, bf16[3,64,4096]{2,1,0:T(8,128)(2,1)} %w_in.1, f32[3,3,64]{2,1,0:T(4,128)} %bitcast.5, bf16[8,8,5120]{2,1,0:T(8,128)(2,1)} %bitcast.4, f32[1,64]{1,0:T(1,128)} %bitcast.7, bf16[64,4096]{1,0:T(8,128)(2,1)} %w_out.1), custom_call_target="tpu_custom_call" | custom-call | tf_op jit(solution)/shard_map/mixer/pallas_call | solution.py:440
  98.0 1.5 %copy.9 = bf16[64,640]{1,0:T(8,128)(2,1)} copy(bf16[64,640]{1,0:T(8,128)(2,1)} %mixer.1) | data formatting | bytes 163840

commit v7 on v4

--- a/solution.py
+++ b/solution.py
@@ -355,7 +355,7 @@
     for b in range(blocks):
         gseq[pl.ds(blocks + b, ROWS, stride=2 * blocks), :] = gated[:, b * LANES : (b + 1) * LANES]
 
-    @pl.loop(0, ROWS, unroll=2)
+    @pl.loop(0, ROWS, unroll=4)
     def _(c):
         base = c * 2 * blocks + blocks
         lhs = jnp.concatenate(

time: 98.3 us -> 98.2 us (level)
  no operation moved by 1% of the time
where the time goes in v7:
time: 98.2 us; the launch traced here: 98 us
  Pallas kernels  96.5 us (98%)
  local copies, waits for them, and re-layouts  1.53 us (2%)
    pallas_call x1, Pallas kernels, shards(): pl.pallas_call(functools.partial(kernel, plan), out_shape=jax.ShapeDtypeS...  96.5 us

profile of v7, /device:TPU:1, one launch (start us, length us, event | category | flops | bytes accessed | tf_op | source)
XLA Modules:
  0.0 98.0 jit_solution(6056935777678737673)
XLA Ops:
  0.0 96.5 %mixer.1 = bf16[64,640]{1,0:T(8,128)(2,1)} custom-call(bf16[64,640]{1,0:T(8,128)(2,1)} %act.1, f32[1,64]{1,0:T(1,128)} %bitcast.6, bf16[3,64,4096]{2,1,0:T(8,128)(2,1)} %w_in.1, f32[3,3,64]{2,1,0:T(4,128)} %bitcast.5, bf16[8,8,5120]{2,1,0:T(8,128)(2,1)} %bitcast.4, f32[1,64]{1,0:T(1,128)} %bitcast.7, bf16[64,4096]{1,0:T(8,128)(2,1)} %w_out.1), custom_call_target="tpu_custom_call" | custom-call | tf_op jit(solution)/shard_map/mixer/pallas_call | solution.py:440
  96.5 1.5 %copy.9 = bf16[64,640]{1,0:T(8,128)(2,1)} copy(bf16[64,640]{1,0:T(8,128)(2,1)} %mixer.1) | data formatting | bytes 163840
